TPU v7x, 512 devices: a whole 4x4x16 slice. The times are simulated.
512 devices in a mesh: segment: 4 (over y), shard: 16 (over z), stream: 8 (over x, core).
Axes of the slice: x: 4, y: 4, z: 16, core: 2. Of those that a mesh axis runs over, the one named last changes fastest.
Arguments:
- latents: bfloat16 [32, 16, 16, 32, 256], P('stream', 'shard'), parts along dimension 0, may hold values from -6 to 6
- norm_gain: float32 [4, 256], P('segment'), may hold values from 0.25 to 1.75
- time_weight: bfloat16 [4, 3, 256, 256], P('segment'), may hold values from -0.21875 to 0.21875
- space_weight: bfloat16 [4, 9, 256, 256], P('segment'), may hold values from -0.125 to 0.125
- carry_in: bfloat16 [4, 16, 16, 32, 256], P('segment', 'stream', 'shard'), parts along dimension 1, may hold values from -6 to 6
Outputs:
- decoded: bfloat16 [32, 16, 16, 32, 256], P(('stream', 'segment'), 'shard'), parts along dimension 0
- carry_out: bfloat16 [4, 16, 16, 32, 256], P('segment', 'stream', 'shard'), parts along dimension 1
There are 8 independent parts, one for each index of `stream`. A program takes and returns all parts, laid end to end along the dimension named above; an argument that names none is the same for every part. Nothing has to cross between parts.
All inputs are finite; a program needn't handle non-finite values.
Results may differ from a plain program's by a relative error of at most 0.009.
Values may be sent and summed in bfloat16 or wider, within the bound.
No kernel may reach another device: no remote copies, remote signals or barrier semaphores. Data moves between devices by JAX's collectives and lax.ppermute only.
A program may use at most 64 MiB of HBM per device.

v0:
```python
import jax
import jax.numpy as jnp
from jax import lax
from jax.sharding import PartitionSpec as P


def shifted(block, axis, distance):
    devices = range(lax.axis_size(axis))
    route = [(i - distance, i) for i in devices if i - distance in devices]
    return lax.ppermute(block, axis, route)


def normalize(frames_in, gain_row):
    values = frames_in.astype(jnp.float32)
    inverse = lax.rsqrt(jnp.mean(values * values, axis=-1, keepdims=True) + 1e-06)
    return (values * inverse * gain_row).astype(jnp.bfloat16)


def project(frames_in, matrix):
    channels = frames_in.shape[-1]
    product = jnp.dot(frames_in.reshape(-1, channels), matrix, preferred_element_type=jnp.float32)
    return product.reshape(frames_in.shape[:-1] + (matrix.shape[1],))


def spatial(hidden, kernel):
    padded = jnp.pad(hidden, ((0, 0), (1, 1), (1, 1), (0, 0)))
    height = hidden.shape[1]
    across = hidden.shape[2]
    summed = jnp.zeros(hidden.shape, jnp.float32)
    for offset in range(9):
        row_shift = offset // 3
        col_shift = offset % 3
        summed = summed + project(
            padded[:, row_shift : row_shift + height, col_shift : col_shift + across],
            kernel[offset],
        )
    return summed


def body(latents, norm_gain, time_weight, space_weight, carry_in):
    sections = lax.axis_size("segment")
    segment_pos = lax.axis_index("segment")
    block_count = latents.shape[0]
    rounds = block_count + sections - 1
    gain_row = norm_gain[0]
    taps = time_weight[0]
    kernel = space_weight[0]
    frame_shape = latents.shape[1:]
    earlier = carry_in[0]
    arriving = jnp.zeros(frame_shape, jnp.bfloat16)
    finished = []
    for turn in range(rounds):
        if turn < block_count:
            fresh = latents[turn]
        else:
            fresh = jnp.zeros(frame_shape, jnp.bfloat16)
        current = jnp.where(segment_pos == 0, fresh, arriving)
        active = jnp.logical_and(turn - segment_pos >= 0, turn - segment_pos < block_count)
        normed = normalize(current, gain_row)
        by_rows = lax.all_to_all(normed, "shard", split_axis=1, concat_axis=0, tiled=True)
        frame_count = by_rows.shape[0]
        extended = jnp.concatenate([earlier, by_rows], axis=0)
        mixed = project(extended[0:frame_count], taps[0])
        mixed = mixed + project(extended[1 : frame_count + 1], taps[1])
        mixed = mixed + project(extended[2 : frame_count + 2], taps[2])
        row_hidden = jax.nn.silu(mixed).astype(jnp.bfloat16)
        earlier = jnp.where(active, by_rows[frame_count - 2 :], earlier)
        hidden = lax.all_to_all(row_hidden, "shard", split_axis=0, concat_axis=1, tiled=True)
        result = (current.astype(jnp.float32) + spatial(hidden, kernel)).astype(jnp.bfloat16)
        if turn >= sections - 1:
            finished.append(result)
        if turn + 1 < rounds:
            arriving = shifted(result, "segment", 1)
    stacked = jnp.stack(finished)
    delivered = lax.all_to_all(stacked, "segment", split_axis=0, concat_axis=0, tiled=True)
    per_segment = block_count // sections
    decoded = delivered[(sections - 1) * per_segment :]
    carry_out = earlier[None]
    return (decoded, carry_out)


def solution(mesh):
    placed = (
        P("stream", "shard", None, None, None),
        P("segment", None),
        P("segment", None, None, None),
        P("segment", None, None, None),
        P("segment", "stream", "shard", None, None),
    )
    return jax.shard_map(
        body,
        mesh=mesh,
        in_specs=placed,
        out_specs=(
            P(("stream", "segment"), "shard", None, None, None),
            P("segment", "stream", "shard", None, None),
        ),
        check_vma=False,
    )
```

profile of v0, /device:TPU:38, one launch (start us, length us, event | category | flops | bytes accessed | tf_op | source)
XLA Modules:
  0.0 432.6 jit_solution(15415007599045715710)
XLA Ops:
  0.7 1.1 fusion.24
  2.9 32.9 %all_to_all.173 = bf16[1,16,32,256]{3,2,0,1:T(8,128)(2,1)S(1)} all-to-all(bf16[1,16,32,256]{3,2,0,1:T(8,128)(2,1)S(1)} %fusion.205), channel_id=1, replica_groups=mesh['segment'=4,'shard'=16,'stream'=8] {'shard'}, dimensions={1} | all-to-all | bytes 524288 | tf_op jit(solution)/shard_map/all_to_all | solution.py:60
  36.7 23.7 %all_to_all.174 = bf16[16,1,32,256]{3,2,1,0:T(8,128)(2,1)S(1)} all-to-all(bf16[16,1,32,256]{3,2,1,0:T(8,128)(2,1)S(1)} %fusion.51), channel_id=1, replica_groups=mesh['segment'=4,'shard'=16,'stream'=8] {'shard'}, dimensions={0} | all-to-all | bytes 524288 | tf_op jit(solution)/shard_map/all_to_all | solution.py:68
  63.3 3.5 collective-permute-start
  66.8 5.0 %collective-permute-done = bf16[1,16,32,256]{3,2,1,0:T(8,128)(2,1)S(1)} collective-permute-done((bf16[1,16,32,256]{3,2,1,0:T(8,128)(2,1)S(1)}, bf16[1,16,32,256]{3,2,1,0:T(8,128)(2,1)S(1)}, u32[]{:S(2)}, u32[]{:S(2)}) %collective-permute-start) | collective-permute-done | bytes 262176 | tf_op jit(solution)/shard_map/ppermute | solution.py:10
  72.8 7.0 %all-to-all-start.2 = ((bf16[1,16,32,256]{3,2,0,1:T(8,128)(2,1)}), bf16[1,16,32,256]{3,2,0,1:T(8,128)(2,1)S(1)}, u32[]{:S(2)}, u32[]{:S(2)}) async-start(bf16[1,16,32,256]{3,2,0,1:T(8,128)(2,1)} %fusion.204), calls=%async_computation.2 | async-start | bytes 524288 | tf_op jit(solution)/shard_map/all_to_all | solution.py:60
  79.8 17.6 %all-to-all-done.2 = bf16[1,16,32,256]{3,2,0,1:T(8,128)(2,1)S(1)} async-done(((bf16[1,16,32,256]{3,2,0,1:T(8,128)(2,1)}), bf16[1,16,32,256]{3,2,0,1:T(8,128)(2,1)S(1)}, u32[]{:S(2)}, u32[]{:S(2)}) %all-to-all-start.2) | async-done | bytes 262176 | tf_op jit(solution)/shard_map/all_to_all | solution.py:60
  98.2 23.3 %all_to_all.175 = bf16[16,1,32,256]{3,2,1,0:T(8,128)(2,1)S(1)} all-to-all(bf16[16,1,32,256]{3,2,1,0:T(8,128)(2,1)S(1)} %fusion.50), channel_id=1, replica_groups=mesh['segment'=4,'shard'=16,'stream'=8] {'shard'}, dimensions={0} | all-to-all | bytes 524288 | tf_op jit(solution)/shard_map/all_to_all | solution.py:68
  123.7 4.4 %collective-permute-start.1 = (bf16[1,16,32,256]{3,2,1,0:T(8,128)(2,1)S(1)}, bf16[1,16,32,256]{3,2,1,0:T(8,128)(2,1)S(1)}, u32[]{:S(2)}, u32[]{:S(2)}) collective-permute-start(bf16[1,16,32,256]{3,2,1,0:T(8,128)(2,1)S(1)} %fusion.18), channel_id=1, source_target_pairs={{0,128},{128,256},{256,384},{1,129},{129,257},{257,385},{2,130},{1... | collective-permute-start | bytes 786440 | tf_op jit(solution)/shard_map/ppermute | solution.py:10
  128.1 3.9 collective-permute-done.1
  132.2 22.7 %all_to_all.176 = bf16[1,16,32,256]{3,2,0,1:T(8,128)(2,1)S(1)} all-to-all(bf16[1,16,32,256]{3,2,0,1:T(8,128)(2,1)S(1)} %fusion.203), channel_id=1, replica_groups=mesh['segment'=4,'shard'=16,'stream'=8] {'shard'}, dimensions={1} | all-to-all | bytes 524288 | tf_op jit(solution)/shard_map/all_to_all | solution.py:60
  155.7 22.5 %all_to_all.177 = bf16[16,1,32,256]{3,2,1,0:T(8,128)(2,1)S(1)} all-to-all(bf16[16,1,32,256]{3,2,1,0:T(8,128)(2,1)S(1)} %fusion.49), channel_id=1, replica_groups=mesh['segment'=4,'shard'=16,'stream'=8] {'shard'}, dimensions={0} | all-to-all | bytes 524288 | tf_op jit(solution)/shard_map/all_to_all | solution.py:68
  180.3 4.4 %collective-permute-start.2 = (bf16[1,16,32,256]{3,2,1,0:T(8,128)(2,1)S(1)}, bf16[1,16,32,256]{3,2,1,0:T(8,128)(2,1)S(1)}, u32[]{:S(2)}, u32[]{:S(2)}) collective-permute-start(bf16[1,16,32,256]{3,2,1,0:T(8,128)(2,1)S(1)} %fusion.17), channel_id=1, source_target_pairs={{0,128},{128,256},{256,384},{1,129},{129,257},{257,385},{2,130},{1... | collective-permute-start | bytes 786440 | tf_op jit(solution)/shard_map/ppermute | solution.py:10
  184.7 4.5 %collective-permute-done.2 = bf16[1,16,32,256]{3,2,1,0:T(8,128)(2,1)S(1)} collective-permute-done((bf16[1,16,32,256]{3,2,1,0:T(8,128)(2,1)S(1)}, bf16[1,16,32,256]{3,2,1,0:T(8,128)(2,1)S(1)}, u32[]{:S(2)}, u32[]{:S(2)}) %collective-permute-start.2) | collective-permute-done | bytes 262176 | tf_op jit(solution)/shard_map/ppermute | solution.py:10
  191.0 6.2 %all-to-all-start.6 = ((bf16[1,16,32,256]{3,2,0,1:T(8,128)(2,1)}), bf16[1,16,32,256]{3,2,0,1:T(8,128)(2,1)S(1)}, u32[]{:S(2)}, u32[]{:S(2)}) async-start(bf16[1,16,32,256]{3,2,0,1:T(8,128)(2,1)} %fusion.202), calls=%async_computation.6 | async-start | bytes 524288 | tf_op jit(solution)/shard_map/all_to_all | solution.py:60
  197.2 17.7 %all-to-all-done.6 = bf16[1,16,32,256]{3,2,0,1:T(8,128)(2,1)S(1)} async-done(((bf16[1,16,32,256]{3,2,0,1:T(8,128)(2,1)}), bf16[1,16,32,256]{3,2,0,1:T(8,128)(2,1)S(1)}, u32[]{:S(2)}, u32[]{:S(2)}) %all-to-all-start.6) | async-done | bytes 262176 | tf_op jit(solution)/shard_map/all_to_all | solution.py:60
  215.7 22.5 %all_to_all.178 = bf16[16,1,32,256]{3,2,1,0:T(8,128)(2,1)S(1)} all-to-all(bf16[16,1,32,256]{3,2,1,0:T(8,128)(2,1)S(1)} %fusion.48), channel_id=1, replica_groups=mesh['segment'=4,'shard'=16,'stream'=8] {'shard'}, dimensions={0} | all-to-all | bytes 524288 | tf_op jit(solution)/shard_map/all_to_all | solution.py:68
  240.8 4.5 %collective-permute-start.3 = (bf16[1,16,32,256]{3,2,1,0:T(8,128)(2,1)S(1)}, bf16[1,16,32,256]{3,2,1,0:T(8,128)(2,1)S(1)}, u32[]{:S(2)}, u32[]{:S(2)}) collective-permute-start(bf16[1,16,32,256]{3,2,1,0:T(8,128)(2,1)S(1)} %fusion.16), channel_id=1, source_target_pairs={{0,128},{128,256},{256,384},{1,129},{129,257},{257,385},{2,130},{1... | collective-permute-start | bytes 786440 | tf_op jit(solution)/shard_map/ppermute | solution.py:10
  245.3 3.9 collective-permute-done.3
  249.5 21.6 %all_to_all.179 = bf16[1,16,32,256]{3,2,0,1:T(8,128)(2,1)S(1)} all-to-all(bf16[1,16,32,256]{3,2,0,1:T(8,128)(2,1)S(1)} %fusion.201), channel_id=1, replica_groups=mesh['segment'=4,'shard'=16,'stream'=8] {'shard'}, dimensions={1} | all-to-all | bytes 524288 | tf_op jit(solution)/shard_map/all_to_all | solution.py:60
  272.0 22.3 %all_to_all.180 = bf16[16,1,32,256]{3,2,1,0:T(8,128)(2,1)S(1)} all-to-all(bf16[16,1,32,256]{3,2,1,0:T(8,128)(2,1)S(1)} %fusion.47), channel_id=1, replica_groups=mesh['segment'=4,'shard'=16,'stream'=8] {'shard'}, dimensions={0} | all-to-all | bytes 524288 | tf_op jit(solution)/shard_map/all_to_all | solution.py:68
  296.4 4.5 %collective-permute-start.4 = (bf16[1,16,32,256]{3,2,1,0:T(8,128)(2,1)S(1)}, bf16[1,16,32,256]{3,2,1,0:T(8,128)(2,1)S(1)}, u32[]{:S(2)}, u32[]{:S(2)}) collective-permute-start(bf16[1,16,32,256]{3,2,1,0:T(8,128)(2,1)S(1)} %fusion.15), channel_id=1, source_target_pairs={{0,128},{128,256},{256,384},{1,129},{129,257},{257,385},{2,130},{1... | collective-permute-start | bytes 786440 | tf_op jit(solution)/shard_map/ppermute | solution.py:10
  300.9 3.9 collective-permute-done.4
  305.8 6.0 %all-to-all-start.10 = ((bf16[1,16,32,256]{3,2,0,1:T(8,128)(2,1)}), bf16[1,16,32,256]{3,2,0,1:T(8,128)(2,1)S(1)}, u32[]{:S(2)}, u32[]{:S(2)}) async-start(bf16[1,16,32,256]{3,2,0,1:T(8,128)(2,1)} %fusion.200), calls=%async_computation.10 | async-start | bytes 524288 | tf_op jit(solution)/shard_map/all_to_all | solution.py:60
  311.8 17.6 %all-to-all-done.10 = bf16[1,16,32,256]{3,2,0,1:T(8,128)(2,1)S(1)} async-done(((bf16[1,16,32,256]{3,2,0,1:T(8,128)(2,1)}), bf16[1,16,32,256]{3,2,0,1:T(8,128)(2,1)S(1)}, u32[]{:S(2)}, u32[]{:S(2)}) %all-to-all-start.10) | async-done | bytes 262176 | tf_op jit(solution)/shard_map/all_to_all | solution.py:60
  330.2 22.4 %all_to_all.181 = bf16[16,1,32,256]{3,2,1,0:T(8,128)(2,1)S(1)} all-to-all(bf16[16,1,32,256]{3,2,1,0:T(8,128)(2,1)S(1)} %fusion.46), channel_id=1, replica_groups=mesh['segment'=4,'shard'=16,'stream'=8] {'shard'}, dimensions={0} | all-to-all | bytes 524288 | tf_op jit(solution)/shard_map/all_to_all | solution.py:68
  354.8 4.4 %collective-permute-start.5 = (bf16[1,16,32,256]{3,2,1,0:T(8,128)(2,1)S(1)}, bf16[1,16,32,256]{3,2,1,0:T(8,128)(2,1)S(1)}, u32[]{:S(2)}, u32[]{:S(2)}) collective-permute-start(bf16[1,16,32,256]{3,2,1,0:T(8,128)(2,1)S(1)} %fusion.14), channel_id=1, source_target_pairs={{0,128},{128,256},{256,384},{1,129},{129,257},{257,385},{2,130},{1... | collective-permute-start | bytes 786440 | tf_op jit(solution)/shard_map/ppermute | solution.py:10
  359.2 4.5 %collective-permute-done.5 = bf16[1,16,32,256]{3,2,1,0:T(8,128)(2,1)S(1)} collective-permute-done((bf16[1,16,32,256]{3,2,1,0:T(8,128)(2,1)S(1)}, bf16[1,16,32,256]{3,2,1,0:T(8,128)(2,1)S(1)}, u32[]{:S(2)}, u32[]{:S(2)}) %collective-permute-start.5) | collective-permute-done | bytes 262176 | tf_op jit(solution)/shard_map/ppermute | solution.py:10
  364.0 23.7 %all_to_all.182 = bf16[1,16,32,256]{3,2,0,1:T(8,128)(2,1)S(1)} all-to-all(bf16[1,16,32,256]{3,2,0,1:T(8,128)(2,1)S(1)} %fusion.199), channel_id=1, replica_groups=mesh['segment'=4,'shard'=16,'stream'=8] {'shard'}, dimensions={1} | all-to-all | bytes 524288 | tf_op jit(solution)/shard_map/all_to_all | solution.py:60
  388.5 22.5 %all_to_all.183 = bf16[16,1,32,256]{3,2,1,0:T(8,128)(2,1)S(1)} all-to-all(bf16[16,1,32,256]{3,2,1,0:T(8,128)(2,1)S(1)} %fusion.45), channel_id=1, replica_groups=mesh['segment'=4,'shard'=16,'stream'=8] {'shard'}, dimensions={0} | all-to-all | bytes 524288 | tf_op jit(solution)/shard_map/all_to_all | solution.py:68
  414.8 6.2 %all-to-all-start.14 = ((bf16[4,1,16,32,256]{4,3,2,1,0:T(8,128)(2,1)}), bf16[4,1,16,32,256]{4,3,2,1,0:T(8,128)(2,1)S(1)}, u32[]{:S(2)}, u32[]{:S(2)}) async-start(bf16[4,1,16,32,256]{4,3,2,1,0:T(8,128)(2,1)} %pad_maximum_fusion), calls=%async_computation.14 | async-start | bytes 2097152 | tf_op jit(solution)/shard_map/all_to_all | solution.py:75
  421.7 10.3 %all-to-all-done.14 = bf16[4,1,16,32,256]{4,3,2,1,0:T(8,128)(2,1)S(1)} async-done(((bf16[4,1,16,32,256]{4,3,2,1,0:T(8,128)(2,1)}), bf16[4,1,16,32,256]{4,3,2,1,0:T(8,128)(2,1)S(1)}, u32[]{:S(2)}, u32[]{:S(2)}) %all-to-all-start.14) | async-done | bytes 1048608 | tf_op jit(solution)/shard_map/all_to_all | solution.py:75
  (132 shorter events, 30.0 us)
Async XLA Ops:
  0.6 35.2 %copy-start.1 = (bf16[1,3,256,256]{3,2,1,0:T(8,128)(2,1)S(1)}, bf16[1,3,256,256]{3,2,1,0:T(8,128)(2,1)}, u32[]{:S(2)}) copy-start(bf16[1,3,256,256]{3,2,1,0:T(8,128)(2,1)} %param.7) | copy-start | bytes 1179652
  0.6 35.2 %copy-start.9 = (bf16[1,2,1,32,256]{4,3,2,1,0:T(8,128)(2,1)S(1)}, bf16[1,2,1,32,256]{4,3,2,1,0:T(8,128)(2,1)}, u32[]{:S(2)}) copy-start(bf16[1,2,1,32,256]{4,3,2,1,0:T(8,128)(2,1)} %param.9) | copy-start | bytes 98308
  36.3 24.1 %copy-start = (bf16[1,9,256,256]{3,2,1,0:T(8,128)(2,1)S(1)}, bf16[1,9,256,256]{3,2,1,0:T(8,128)(2,1)}, u32[]{:S(2)}) copy-start(bf16[1,9,256,256]{3,2,1,0:T(8,128)(2,1)} %param.8) | copy-start | bytes 3538948
  61.8 1.2 copy-start.2
  63.1 8.9 %copy-start.10 = (f32[1,256]{1,0:T(1,128)S(1)}, f32[1,256]{1,0:T(1,128)}, u32[]{:S(2)}) copy-start(f32[1,256]{1,0:T(1,128)} %param.6) | copy-start | bytes 3076
  63.3 8.5 %collective-permute-start = (bf16[1,16,32,256]{3,2,1,0:T(8,128)(2,1)S(1)}, bf16[1,16,32,256]{3,2,1,0:T(8,128)(2,1)S(1)}, u32[]{:S(2)}, u32[]{:S(2)}) collective-permute-start(bf16[1,16,32,256]{3,2,1,0:T(8,128)(2,1)S(1)} %fusion.20), channel_id=1, source_target_pairs={{0,128},{128,256},{256,384},{1,129},{129,257},{257,385},{2,130},{1... | collective-permute-start | bytes 786440 | tf_op jit(solution)/shard_map/ppermute | solution.py:10
  72.8 24.6 %all-to-all-start.2 = ((bf16[1,16,32,256]{3,2,0,1:T(8,128)(2,1)}), bf16[1,16,32,256]{3,2,0,1:T(8,128)(2,1)S(1)}, u32[]{:S(2)}, u32[]{:S(2)}) async-start(bf16[1,16,32,256]{3,2,0,1:T(8,128)(2,1)} %fusion.204), calls=%async_computation.2 | async-start | bytes 524288 | tf_op jit(solution)/shard_map/all_to_all | solution.py:60
  123.7 8.2 %collective-permute-start.1 = (bf16[1,16,32,256]{3,2,1,0:T(8,128)(2,1)S(1)}, bf16[1,16,32,256]{3,2,1,0:T(8,128)(2,1)S(1)}, u32[]{:S(2)}, u32[]{:S(2)}) collective-permute-start(bf16[1,16,32,256]{3,2,1,0:T(8,128)(2,1)S(1)} %fusion.18), channel_id=1, source_target_pairs={{0,128},{128,256},{256,384},{1,129},{129,257},{257,385},{2,130},{1... | collective-permute-start | bytes 786440 | tf_op jit(solution)/shard_map/ppermute | solution.py:10
  180.3 8.9 %collective-permute-start.2 = (bf16[1,16,32,256]{3,2,1,0:T(8,128)(2,1)S(1)}, bf16[1,16,32,256]{3,2,1,0:T(8,128)(2,1)S(1)}, u32[]{:S(2)}, u32[]{:S(2)}) collective-permute-start(bf16[1,16,32,256]{3,2,1,0:T(8,128)(2,1)S(1)} %fusion.17), channel_id=1, source_target_pairs={{0,128},{128,256},{256,384},{1,129},{129,257},{257,385},{2,130},{1... | collective-permute-start | bytes 786440 | tf_op jit(solution)/shard_map/ppermute | solution.py:10
  189.4 0.7 copy-start.3
  191.0 23.9 %all-to-all-start.6 = ((bf16[1,16,32,256]{3,2,0,1:T(8,128)(2,1)}), bf16[1,16,32,256]{3,2,0,1:T(8,128)(2,1)S(1)}, u32[]{:S(2)}, u32[]{:S(2)}) async-start(bf16[1,16,32,256]{3,2,0,1:T(8,128)(2,1)} %fusion.202), calls=%async_computation.6 | async-start | bytes 524288 | tf_op jit(solution)/shard_map/all_to_all | solution.py:60
  239.6 1.0 copy-start.4
  240.8 30.9 %copy-start.5 = (bf16[1,16,32,256]{3,2,1,0:T(8,128)(2,1)}, bf16[1,16,32,256]{3,2,1,0:T(8,128)(2,1)S(1)}, u32[]{:S(2)}) copy-start(bf16[1,16,32,256]{3,2,1,0:T(8,128)(2,1)S(1)} %fusion.16) | copy-start | bytes 786436
  240.8 8.4 %collective-permute-start.3 = (bf16[1,16,32,256]{3,2,1,0:T(8,128)(2,1)S(1)}, bf16[1,16,32,256]{3,2,1,0:T(8,128)(2,1)S(1)}, u32[]{:S(2)}, u32[]{:S(2)}) collective-permute-start(bf16[1,16,32,256]{3,2,1,0:T(8,128)(2,1)S(1)} %fusion.16), channel_id=1, source_target_pairs={{0,128},{128,256},{256,384},{1,129},{129,257},{257,385},{2,130},{1... | collective-permute-start | bytes 786440 | tf_op jit(solution)/shard_map/ppermute | solution.py:10
  296.4 9.4 %copy-start.7 = (bf16[1,16,32,256]{3,2,1,0:T(8,128)(2,1)}, bf16[1,16,32,256]{3,2,1,0:T(8,128)(2,1)S(1)}, u32[]{:S(2)}) copy-start(bf16[1,16,32,256]{3,2,1,0:T(8,128)(2,1)S(1)} %fusion.15) | copy-start | bytes 786436
  296.4 8.4 %collective-permute-start.4 = (bf16[1,16,32,256]{3,2,1,0:T(8,128)(2,1)S(1)}, bf16[1,16,32,256]{3,2,1,0:T(8,128)(2,1)S(1)}, u32[]{:S(2)}, u32[]{:S(2)}) collective-permute-start(bf16[1,16,32,256]{3,2,1,0:T(8,128)(2,1)S(1)} %fusion.15), channel_id=1, source_target_pairs={{0,128},{128,256},{256,384},{1,129},{129,257},{257,385},{2,130},{1... | collective-permute-start | bytes 786440 | tf_op jit(solution)/shard_map/ppermute | solution.py:10
  305.8 23.6 %all-to-all-start.10 = ((bf16[1,16,32,256]{3,2,0,1:T(8,128)(2,1)}), bf16[1,16,32,256]{3,2,0,1:T(8,128)(2,1)S(1)}, u32[]{:S(2)}, u32[]{:S(2)}) async-start(bf16[1,16,32,256]{3,2,0,1:T(8,128)(2,1)} %fusion.200), calls=%async_computation.10 | async-start | bytes 524288 | tf_op jit(solution)/shard_map/all_to_all | solution.py:60
  354.8 8.9 %collective-permute-start.5 = (bf16[1,16,32,256]{3,2,1,0:T(8,128)(2,1)S(1)}, bf16[1,16,32,256]{3,2,1,0:T(8,128)(2,1)S(1)}, u32[]{:S(2)}, u32[]{:S(2)}) collective-permute-start(bf16[1,16,32,256]{3,2,1,0:T(8,128)(2,1)S(1)} %fusion.14), channel_id=1, source_target_pairs={{0,128},{128,256},{256,384},{1,129},{129,257},{257,385},{2,130},{1... | collective-permute-start | bytes 786440 | tf_op jit(solution)/shard_map/ppermute | solution.py:10
  412.6 1.0 copy-start.6
  412.7 1.0 copy-start.8
  414.8 17.1 %all-to-all-start.14 = ((bf16[4,1,16,32,256]{4,3,2,1,0:T(8,128)(2,1)}), bf16[4,1,16,32,256]{4,3,2,1,0:T(8,128)(2,1)S(1)}, u32[]{:S(2)}, u32[]{:S(2)}) async-start(bf16[4,1,16,32,256]{4,3,2,1,0:T(8,128)(2,1)} %pad_maximum_fusion), calls=%async_computation.14 | async-start | bytes 2097152 | tf_op jit(solution)/shard_map/all_to_all | solution.py:75
where the time goes:
time: 434 us; the launch traced here: 433 us
  blocking collectives  260 us (60%)
  waiting for transfers between devices  88.7 us (20%)
  starting transfers between devices  51.3 us (12%)
  matrix products  20 us (5%)
  other arithmetic  7.9 us (2%)
    all_to_all x7, blocking collectives, body(): lax.all_to_all(row_hidden, 'shard', split_axis=0, concat_axis=1, tiled=True)  159 us
    all_to_all x4, blocking collectives, body(): lax.all_to_all(normed, 'shard', split_axis=1, concat_axis=0, tiled=True)  101 us
    all_to_all x3, waiting for transfers between devices, body(): lax.all_to_all(normed, 'shard', split_axis=1, concat_axis=0, tiled=True)  52.9 us
    ppermute x6, starting transfers between devices, shifted(): return lax.ppermute(block, axis, route)  25.8 us
    ppermute x6, waiting for transfers between devices, shifted(): return lax.ppermute(block, axis, route)  25.6 us
    dot_general x84, matrix products, project(): jnp.dot(frames_in.reshape(-1, channels), matrix, preferred_element_type=j...  20 us
    all_to_all x3, starting transfers between devices, body(): lax.all_to_all(normed, 'shard', split_axis=1, concat_axis=0, tiled=True)  19.2 us
    all_to_all x1, waiting for transfers between devices, body(): lax.all_to_all(stacked, 'segment', split_axis=0, concat_axis=0, tiled=True)  10.3 us
  transfers between devices with their start and end apart: 10, of which 10 were waited for; matrix products, arithmetic and copies ran while one was open for 0% of the time, Pallas kernels for 0%

commit v1 on v0

--- a/solution.py
+++ b/solution.py
@@ -57,7 +57,12 @@
         current = jnp.where(segment_pos == 0, fresh, arriving)
         active = jnp.logical_and(turn - segment_pos >= 0, turn - segment_pos < block_count)
         normed = normalize(current, gain_row)
-        by_rows = lax.all_to_all(normed, "shard", split_axis=1, concat_axis=0, tiled=True)
+        by_rows = jnp.concatenate(
+            lax.all_to_all(
+                jnp.stack(jnp.split(normed, lax.axis_size("shard"), axis=1)), "shard", 0, 0
+            ),
+            axis=0,
+        )
         frame_count = by_rows.shape[0]
         extended = jnp.concatenate([earlier, by_rows], axis=0)
         mixed = project(extended[0:frame_count], taps[0])

time: 434 us -> 463 us (1.067)
  the two profiles are of different devices: /device:TPU:38 before, /device:TPU:32 now
where the time goes in v1:
time: 463 us; the launch traced here: 462 us
  blocking collectives  261 us (56%)
  waiting for transfers between devices  92 us (20%)
  starting transfers between devices  48.5 us (10%)
  local copies, waits for them, and re-layouts  32.5 us (7%)
  matrix products  20 us (4%)
  other arithmetic  5.78 us (1%)
    all_to_all x7, blocking collectives, body(): lax.all_to_all(row_hidden, 'shard', split_axis=0, concat_axis=1, tiled=True)  159 us
    all_to_all x4, blocking collectives, body(): lax.all_to_all(jnp.stack(jnp.split(normed, lax.axis_size('shard'), axis=1...  102 us
    all_to_all x3, waiting for transfers between devices, body(): lax.all_to_all(jnp.stack(jnp.split(normed, lax.axis_size('shard'), axis=1...  52.7 us
    unnamed x127, local copies, waits for them, and re-layouts  30 us
    ppermute x6, waiting for transfers between devices, shifted(): return lax.ppermute(block, axis, route)  26.1 us
    ppermute x6, starting transfers between devices, shifted(): return lax.ppermute(block, axis, route)  25.5 us
    dot_general x84, matrix products, project(): jnp.dot(frames_in.reshape(-1, channels), matrix, preferred_element_type=j...  20 us
    all_to_all x3, starting transfers between devices, body(): lax.all_to_all(jnp.stack(jnp.split(normed, lax.axis_size('shard'), axis=1...  19.2 us
  transfers between devices with their start and end apart: 10, of which 10 were waited for; matrix products, arithmetic and copies ran while one was open for 0% of the time, Pallas kernels for 0%

profile of v1, /device:TPU:32, one launch (start us, length us, event | category | flops | bytes accessed | tf_op | source)
XLA Modules:
  0.0 461.6 jit_solution(8077085484896885736)
XLA Ops:
  0.7 1.1 fusion.24
  3.1 32.9 %all_to_all.124 = bf16[16,1,1,32,256]{4,3,2,1,0:T(8,128)(2,1)S(1)} all-to-all(bf16[16,1,1,32,256]{4,3,2,1,0:T(8,128)(2,1)S(1)} %constant_dynamic-update-slice_fusion), channel_id=1, replica_groups=mesh['segment'=4,'shard'=16,'stream'=8] {'shard'}, dimensions={0} | all-to-all | bytes 524288 | tf_op jit(solution)/shard_map/all_to_all | solution.py:61
  36.8 23.7 %all_to_all.125 = bf16[16,1,32,256]{3,2,1,0:T(8,128)(2,1)S(1)} all-to-all(bf16[16,1,32,256]{3,2,1,0:T(8,128)(2,1)S(1)} %fusion.51), channel_id=1, replica_groups=mesh['segment'=4,'shard'=16,'stream'=8] {'shard'}, dimensions={0} | all-to-all | bytes 524288 | tf_op jit(solution)/shard_map/all_to_all | solution.py:73
  63.5 3.5 collective-permute-start
  67.0 5.0 %collective-permute-done = bf16[1,16,32,256]{3,2,1,0:T(8,128)(2,1)S(1)} collective-permute-done((bf16[1,16,32,256]{3,2,1,0:T(8,128)(2,1)S(1)}, bf16[1,16,32,256]{3,2,1,0:T(8,128)(2,1)S(1)}, u32[]{:S(2)}, u32[]{:S(2)}) %collective-permute-start) | collective-permute-done | bytes 262176 | tf_op jit(solution)/shard_map/ppermute | solution.py:10
  82.0 7.0 %all-to-all-start.2 = ((bf16[16,1,1,32,256]{4,3,2,1,0:T(8,128)(2,1)}), bf16[16,1,1,32,256]{4,3,2,1,0:T(8,128)(2,1)S(1)}, u32[]{:S(2)}, u32[]{:S(2)}) async-start(bf16[16,1,1,32,256]{4,3,2,1,0:T(8,128)(2,1)} %constant_dynamic-update-slice_fusion.16), calls=%async_computation.2 | async-start | bytes 524288 | tf_op jit(solution)/shard_map/all_to_all | solution.py:61
  89.0 17.6 %all-to-all-done.2 = bf16[16,1,1,32,256]{4,3,2,1,0:T(8,128)(2,1)S(1)} async-done(((bf16[16,1,1,32,256]{4,3,2,1,0:T(8,128)(2,1)}), bf16[16,1,1,32,256]{4,3,2,1,0:T(8,128)(2,1)S(1)}, u32[]{:S(2)}, u32[]{:S(2)}) %all-to-all-start.2) | async-done | bytes 262176 | tf_op jit(solution)/shard_map/all_to_all | solution.py:61
  107.4 23.0 %all_to_all.126 = bf16[16,1,32,256]{3,2,1,0:T(8,128)(2,1)S(1)} all-to-all(bf16[16,1,32,256]{3,2,1,0:T(8,128)(2,1)S(1)} %fusion.50), channel_id=1, replica_groups=mesh['segment'=4,'shard'=16,'stream'=8] {'shard'}, dimensions={0} | all-to-all | bytes 524288 | tf_op jit(solution)/shard_map/all_to_all | solution.py:73
  132.5 4.4 collective-permute-start.1
  136.9 4.4 collective-permute-done.1
  141.8 23.4 %all_to_all.127 = bf16[16,1,1,32,256]{4,3,2,1,0:T(8,128)(2,1)S(1)} all-to-all(bf16[16,1,1,32,256]{4,3,2,1,0:T(8,128)(2,1)S(1)} %constant_dynamic-update-slice_fusion.32), channel_id=1, replica_groups=mesh['segment'=4,'shard'=16,'stream'=8] {'shard'}, dimensions={0} | all-to-all | bytes 524288 | tf_op jit(solution)/shard_map/all_to_all | solution.py:61
  166.0 22.4 %all_to_all.128 = bf16[16,1,32,256]{3,2,1,0:T(8,128)(2,1)S(1)} all-to-all(bf16[16,1,32,256]{3,2,1,0:T(8,128)(2,1)S(1)} %fusion.49), channel_id=1, replica_groups=mesh['segment'=4,'shard'=16,'stream'=8] {'shard'}, dimensions={0} | all-to-all | bytes 524288 | tf_op jit(solution)/shard_map/all_to_all | solution.py:73
  190.6 4.4 collective-permute-start.2
  195.0 4.5 collective-permute-done.2
  210.2 6.3 %all-to-all-start.6 = ((bf16[16,1,1,32,256]{4,3,2,1,0:T(8,128)(2,1)}), bf16[16,1,1,32,256]{4,3,2,1,0:T(8,128)(2,1)S(1)}, u32[]{:S(2)}, u32[]{:S(2)}) async-start(bf16[16,1,1,32,256]{4,3,2,1,0:T(8,128)(2,1)} %constant_dynamic-update-slice_fusion.48), calls=%async_computation.6 | async-start | bytes 524288 | tf_op jit(solution)/shard_map/all_to_all | solution.py:61
  216.6 17.7 %all-to-all-done.6 = bf16[16,1,1,32,256]{4,3,2,1,0:T(8,128)(2,1)S(1)} async-done(((bf16[16,1,1,32,256]{4,3,2,1,0:T(8,128)(2,1)}), bf16[16,1,1,32,256]{4,3,2,1,0:T(8,128)(2,1)S(1)}, u32[]{:S(2)}, u32[]{:S(2)}) %all-to-all-start.6) | async-done | bytes 262176 | tf_op jit(solution)/shard_map/all_to_all | solution.py:61
  235.0 22.5 %all_to_all.129 = bf16[16,1,32,256]{3,2,1,0:T(8,128)(2,1)S(1)} all-to-all(bf16[16,1,32,256]{3,2,1,0:T(8,128)(2,1)S(1)} %fusion.48), channel_id=1, replica_groups=mesh['segment'=4,'shard'=16,'stream'=8] {'shard'}, dimensions={0} | all-to-all | bytes 524288 | tf_op jit(solution)/shard_map/all_to_all | solution.py:73
  260.2 4.4 collective-permute-start.3
  264.6 3.9 collective-permute-done.3
  268.9 21.7 %all_to_all.130 = bf16[16,1,1,32,256]{4,3,2,1,0:T(8,128)(2,1)S(1)} all-to-all(bf16[16,1,1,32,256]{4,3,2,1,0:T(8,128)(2,1)S(1)} %constant_dynamic-update-slice_fusion.64), channel_id=1, replica_groups=mesh['segment'=4,'shard'=16,'stream'=8] {'shard'}, dimensions={0} | all-to-all | bytes 524288 | tf_op jit(solution)/shard_map/all_to_all | solution.py:61
  291.4 22.3 %all_to_all.131 = bf16[16,1,32,256]{3,2,1,0:T(8,128)(2,1)S(1)} all-to-all(bf16[16,1,32,256]{3,2,1,0:T(8,128)(2,1)S(1)} %fusion.47), channel_id=1, replica_groups=mesh['segment'=4,'shard'=16,'stream'=8] {'shard'}, dimensions={0} | all-to-all | bytes 524288 | tf_op jit(solution)/shard_map/all_to_all | solution.py:73
  315.8 4.4 collective-permute-start.4
  320.3 3.9 collective-permute-done.4
  334.1 5.9 %all-to-all-start.10 = ((bf16[16,1,1,32,256]{4,3,2,1,0:T(8,128)(2,1)}), bf16[16,1,1,32,256]{4,3,2,1,0:T(8,128)(2,1)S(1)}, u32[]{:S(2)}, u32[]{:S(2)}) async-start(bf16[16,1,1,32,256]{4,3,2,1,0:T(8,128)(2,1)} %constant_dynamic-update-slice_fusion.80), calls=%async_computation.10 | async-start | bytes 524288 | tf_op jit(solution)/shard_map/all_to_all | solution.py:61
  340.0 17.5 %all-to-all-done.10 = bf16[16,1,1,32,256]{4,3,2,1,0:T(8,128)(2,1)S(1)} async-done(((bf16[16,1,1,32,256]{4,3,2,1,0:T(8,128)(2,1)}), bf16[16,1,1,32,256]{4,3,2,1,0:T(8,128)(2,1)S(1)}, u32[]{:S(2)}, u32[]{:S(2)}) %all-to-all-start.10) | async-done | bytes 262176 | tf_op jit(solution)/shard_map/all_to_all | solution.py:61
  358.3 22.4 %all_to_all.132 = bf16[16,1,32,256]{3,2,1,0:T(8,128)(2,1)S(1)} all-to-all(bf16[16,1,32,256]{3,2,1,0:T(8,128)(2,1)S(1)} %fusion.46), channel_id=1, replica_groups=mesh['segment'=4,'shard'=16,'stream'=8] {'shard'}, dimensions={0} | all-to-all | bytes 524288 | tf_op jit(solution)/shard_map/all_to_all | solution.py:73
  382.9 4.4 collective-permute-start.5
  387.3 4.5 collective-permute-done.5
  392.3 23.8 %all_to_all.133 = bf16[16,1,1,32,256]{4,3,2,1,0:T(8,128)(2,1)S(1)} all-to-all(bf16[16,1,1,32,256]{4,3,2,1,0:T(8,128)(2,1)S(1)} %constant_dynamic-update-slice_fusion.96), channel_id=1, replica_groups=mesh['segment'=4,'shard'=16,'stream'=8] {'shard'}, dimensions={0} | all-to-all | bytes 524288 | tf_op jit(solution)/shard_map/all_to_all | solution.py:61
  416.9 22.5 %all_to_all.134 = bf16[16,1,32,256]{3,2,1,0:T(8,128)(2,1)S(1)} all-to-all(bf16[16,1,32,256]{3,2,1,0:T(8,128)(2,1)S(1)} %fusion.45), channel_id=1, replica_groups=mesh['segment'=4,'shard'=16,'stream'=8] {'shard'}, dimensions={0} | all-to-all | bytes 524288 | tf_op jit(solution)/shard_map/all_to_all | solution.py:73
  443.2 3.7 all-to-all-start.14
  447.6 13.3 %all-to-all-done.14 = bf16[4,1,16,32,256]{4,3,2,1,0:T(8,128)(2,1)S(1)} async-done(((bf16[4,1,16,32,256]{4,3,2,1,0:T(8,128)(2,1)}), bf16[4,1,16,32,256]{4,3,2,1,0:T(8,128)(2,1)S(1)}, u32[]{:S(2)}, u32[]{:S(2)}) %all-to-all-start.14) | async-done | bytes 1048608 | tf_op jit(solution)/shard_map/all_to_all | solution.py:80
  (244 shorter events, 57.2 us)
Async XLA Ops:
  0.6 35.4 %copy-start.1 = (bf16[1,3,256,256]{3,2,1,0:T(8,128)(2,1)S(1)}, bf16[1,3,256,256]{3,2,1,0:T(8,128)(2,1)}, u32[]{:S(2)}) copy-start(bf16[1,3,256,256]{3,2,1,0:T(8,128)(2,1)} %param.7) | copy-start | bytes 1179652
  0.6 35.4 %copy-start.9 = (bf16[1,2,1,32,256]{4,3,2,1,0:T(8,128)(2,1)S(1)}, bf16[1,2,1,32,256]{4,3,2,1,0:T(8,128)(2,1)}, u32[]{:S(2)}) copy-start(bf16[1,2,1,32,256]{4,3,2,1,0:T(8,128)(2,1)} %param.9) | copy-start | bytes 98308
  36.5 24.1 %copy-start = (bf16[1,9,256,256]{3,2,1,0:T(8,128)(2,1)S(1)}, bf16[1,9,256,256]{3,2,1,0:T(8,128)(2,1)}, u32[]{:S(2)}) copy-start(bf16[1,9,256,256]{3,2,1,0:T(8,128)(2,1)} %param.8) | copy-start | bytes 3538948
  62.0 1.2 copy-start.2
  63.2 8.9 %copy-start.10 = (f32[1,256]{1,0:T(1,128)S(1)}, f32[1,256]{1,0:T(1,128)}, u32[]{:S(2)}) copy-start(f32[1,256]{1,0:T(1,128)} %param.6) | copy-start | bytes 3076
  63.5 8.5 %collective-permute-start = (bf16[1,16,32,256]{3,2,1,0:T(8,128)(2,1)S(1)}, bf16[1,16,32,256]{3,2,1,0:T(8,128)(2,1)S(1)}, u32[]{:S(2)}, u32[]{:S(2)}) collective-permute-start(bf16[1,16,32,256]{3,2,1,0:T(8,128)(2,1)S(1)} %fusion.20), channel_id=1, source_target_pairs={{0,128},{128,256},{256,384},{1,129},{129,257},{257,385},{2,130},{1... | collective-permute-start | bytes 786440 | tf_op jit(solution)/shard_map/ppermute | solution.py:10
  82.0 24.5 %all-to-all-start.2 = ((bf16[16,1,1,32,256]{4,3,2,1,0:T(8,128)(2,1)}), bf16[16,1,1,32,256]{4,3,2,1,0:T(8,128)(2,1)S(1)}, u32[]{:S(2)}, u32[]{:S(2)}) async-start(bf16[16,1,1,32,256]{4,3,2,1,0:T(8,128)(2,1)} %constant_dynamic-update-slice_fusion.16), calls=%async_computation.2 | async-start | bytes 524288 | tf_op jit(solution)/shard_map/all_to_all | solution.py:61
  132.5 8.8 %collective-permute-start.1 = (bf16[1,16,32,256]{3,2,1,0:T(8,128)(2,1)S(1)}, bf16[1,16,32,256]{3,2,1,0:T(8,128)(2,1)S(1)}, u32[]{:S(2)}, u32[]{:S(2)}) collective-permute-start(bf16[1,16,32,256]{3,2,1,0:T(8,128)(2,1)S(1)} %fusion.18), channel_id=1, source_target_pairs={{0,128},{128,256},{256,384},{1,129},{129,257},{257,385},{2,130},{1... | collective-permute-start | bytes 786440 | tf_op jit(solution)/shard_map/ppermute | solution.py:10
  190.6 8.9 %collective-permute-start.2 = (bf16[1,16,32,256]{3,2,1,0:T(8,128)(2,1)S(1)}, bf16[1,16,32,256]{3,2,1,0:T(8,128)(2,1)S(1)}, u32[]{:S(2)}, u32[]{:S(2)}) collective-permute-start(bf16[1,16,32,256]{3,2,1,0:T(8,128)(2,1)S(1)} %fusion.17), channel_id=1, source_target_pairs={{0,128},{128,256},{256,384},{1,129},{129,257},{257,385},{2,130},{1... | collective-permute-start | bytes 786440 | tf_op jit(solution)/shard_map/ppermute | solution.py:10
  199.7 0.7 copy-start.3
  210.2 24.0 %all-to-all-start.6 = ((bf16[16,1,1,32,256]{4,3,2,1,0:T(8,128)(2,1)}), bf16[16,1,1,32,256]{4,3,2,1,0:T(8,128)(2,1)S(1)}, u32[]{:S(2)}, u32[]{:S(2)}) async-start(bf16[16,1,1,32,256]{4,3,2,1,0:T(8,128)(2,1)} %constant_dynamic-update-slice_fusion.48), calls=%async_computation.6 | async-start | bytes 524288 | tf_op jit(solution)/shard_map/all_to_all | solution.py:61
  259.0 1.0 copy-start.4
  260.2 30.6 %copy-start.5 = (bf16[1,16,32,256]{3,2,1,0:T(8,128)(2,1)}, bf16[1,16,32,256]{3,2,1,0:T(8,128)(2,1)S(1)}, u32[]{:S(2)}) copy-start(bf16[1,16,32,256]{3,2,1,0:T(8,128)(2,1)S(1)} %fusion.16) | copy-start | bytes 786436
  260.2 8.2 %collective-permute-start.3 = (bf16[1,16,32,256]{3,2,1,0:T(8,128)(2,1)S(1)}, bf16[1,16,32,256]{3,2,1,0:T(8,128)(2,1)S(1)}, u32[]{:S(2)}, u32[]{:S(2)}) collective-permute-start(bf16[1,16,32,256]{3,2,1,0:T(8,128)(2,1)S(1)} %fusion.16), channel_id=1, source_target_pairs={{0,128},{128,256},{256,384},{1,129},{129,257},{257,385},{2,130},{1... | collective-permute-start | bytes 786440 | tf_op jit(solution)/shard_map/ppermute | solution.py:10
  315.8 8.4 %copy-start.7 = (bf16[1,16,32,256]{3,2,1,0:T(8,128)(2,1)}, bf16[1,16,32,256]{3,2,1,0:T(8,128)(2,1)S(1)}, u32[]{:S(2)}) copy-start(bf16[1,16,32,256]{3,2,1,0:T(8,128)(2,1)S(1)} %fusion.15) | copy-start | bytes 786436
  315.8 8.3 %collective-permute-start.4 = (bf16[1,16,32,256]{3,2,1,0:T(8,128)(2,1)S(1)}, bf16[1,16,32,256]{3,2,1,0:T(8,128)(2,1)S(1)}, u32[]{:S(2)}, u32[]{:S(2)}) collective-permute-start(bf16[1,16,32,256]{3,2,1,0:T(8,128)(2,1)S(1)} %fusion.15), channel_id=1, source_target_pairs={{0,128},{128,256},{256,384},{1,129},{129,257},{257,385},{2,130},{1... | collective-permute-start | bytes 786440 | tf_op jit(solution)/shard_map/ppermute | solution.py:10
  334.1 23.4 %all-to-all-start.10 = ((bf16[16,1,1,32,256]{4,3,2,1,0:T(8,128)(2,1)}), bf16[16,1,1,32,256]{4,3,2,1,0:T(8,128)(2,1)S(1)}, u32[]{:S(2)}, u32[]{:S(2)}) async-start(bf16[16,1,1,32,256]{4,3,2,1,0:T(8,128)(2,1)} %constant_dynamic-update-slice_fusion.80), calls=%async_computation.10 | async-start | bytes 524288 | tf_op jit(solution)/shard_map/all_to_all | solution.py:61
  382.9 8.9 %collective-permute-start.5 = (bf16[1,16,32,256]{3,2,1,0:T(8,128)(2,1)S(1)}, bf16[1,16,32,256]{3,2,1,0:T(8,128)(2,1)S(1)}, u32[]{:S(2)}, u32[]{:S(2)}) collective-permute-start(bf16[1,16,32,256]{3,2,1,0:T(8,128)(2,1)S(1)} %fusion.14), channel_id=1, source_target_pairs={{0,128},{128,256},{256,384},{1,129},{129,257},{257,385},{2,130},{1... | collective-permute-start | bytes 786440 | tf_op jit(solution)/shard_map/ppermute | solution.py:10
  441.1 1.0 copy-start.6
  441.1 1.0 copy-start.8
  443.2 17.6 %all-to-all-start.14 = ((bf16[4,1,16,32,256]{4,3,2,1,0:T(8,128)(2,1)}), bf16[4,1,16,32,256]{4,3,2,1,0:T(8,128)(2,1)S(1)}, u32[]{:S(2)}, u32[]{:S(2)}) async-start(bf16[4,1,16,32,256]{4,3,2,1,0:T(8,128)(2,1)} %pad_maximum_fusion), calls=%async_computation.14 | async-start | bytes 2097152 | tf_op jit(solution)/shard_map/all_to_all | solution.py:80
